TPU v7x, 32 devices: a whole 2x2x4 slice. The times are simulated.
32 devices in a mesh: row: 4 (over y, x), col: 8 (over z, core).
Axes of the slice: x: 2, y: 2, z: 4, core: 2. Of those that a mesh axis runs over, the one named last changes fastest.
Arguments:
- coeffs: bfloat16 [16384, 2048], P('row'), may hold values from -1 to 1
- p_slots: int32 [4, 8, 64], P('row', 'col'), may hold values from 0 to 511, as said below
- p_count: int32 [4, 8], P('row', 'col'), may hold values from 1 to 64
- s_blocks: bfloat16 [4, 8, 64, 128, 128], P('row', 'col'), may hold values from -0.3984375 to 0.3984375
- s_slots: int32 [4, 8, 64], P('row', 'col'), may hold values from 0 to 511, as said below
- s_count: int32 [4, 8], P('row', 'col'), may hold values from 1 to 64
- q_slots: int32 [4, 8, 64], P('row', 'col'), may hold values from 0 to 511, as said below
- q_count: int32 [4, 8], P('row', 'col'), may hold values from 1 to 64
Outputs:
- density: bfloat16 [4, 8, 64, 128, 128], P('row', 'col')
- product: float32 [4, 8, 64, 128, 128], P('row', 'col')
Inputs may be any that keep to these rules, and one draw needn't show every extreme that they name: `p_slots`: on each device the live slots name different blocks of its tile; at least one device has all 64 slots live, which one is drawn. `s_slots`: on each device the live slots name different positions; at least one device has all 64 slots live, which one is drawn. `q_slots`: on each device the live slots name different blocks of its tile; at least one device has all 64 slots live, which one is drawn.
All inputs are finite; a program needn't handle non-finite values.
Results may differ from a plain program's by a relative error of at most 0.0029.
Values may be sent and summed in bfloat16 or wider, within the bound.
No kernel may reach another device: no remote copies, remote signals or barrier semaphores. Data moves between devices by JAX's collectives and lax.ppermute only.
A program may use at most 192 MiB of HBM per device.

v0:
```python
import jax
import jax.numpy as jnp
from jax import lax
from jax.sharding import PartitionSpec as P


def from_root(block, axis, source):
    block = jnp.where(lax.axis_index(axis) == source, block, jnp.zeros_like(block))
    return lax.psum(block, axis)


def shortened(shard):

    def short(part):
        return part.astype(jnp.bfloat16) if part.dtype == jnp.float32 else part

    return jax.tree.map(short, shard)


def shifted(block, axis, distance):
    devices = range(lax.axis_size(axis))
    route = [((i - distance) % len(devices), i) for i in devices]
    return lax.ppermute(block, axis, route)


def step_product(summed, p_data, s_data, panel_slot, q_row, q_col, tile_cols):
    p_blocks, p_code = p_data
    s_blocks, s_code = s_data
    local_k = jnp.arange(tile_cols, dtype=jnp.int32)
    p_live = p_code >= 0
    p_row = jnp.where(p_live, p_code // tile_cols, -1)
    p_col = jnp.where(p_live, p_code % tile_cols, -1)
    pick_left = (
        (p_row[:, None, None] == q_row[None, :, None])
        & (p_col[:, None, None] == local_k[None, None, :])
    ).astype(jnp.bfloat16)
    left_rows = jnp.einsum("pqk,pab->qakb", pick_left, p_blocks, preferred_element_type=jnp.float32)
    left_rows = left_rows.astype(jnp.bfloat16).reshape(q_row.shape[0], 128, tile_cols * 128)
    square = tile_cols * tile_cols
    s_live = (s_code >= 0) & (s_code // square == panel_slot)
    s_local = s_code % square
    s_row = jnp.where(s_live, s_local // tile_cols, -1)
    s_col = s_local % tile_cols
    pick_right = (
        (s_row[:, None, None] == local_k[None, :, None])
        & (s_col[:, None, None] == q_col[None, None, :])
    ).astype(jnp.bfloat16)
    right_cols = jnp.einsum(
        "skq,sab->kaqb", pick_right, s_blocks, preferred_element_type=jnp.float32
    )
    right_cols = right_cols.astype(jnp.bfloat16).reshape(tile_cols * 128, q_row.shape[0], 128)
    return summed + jnp.einsum(
        "qak,kqb->qab", left_rows, right_cols, preferred_element_type=jnp.float32
    )


def pick_tree(flag, moved, kept):
    return jax.tree.map(lambda fresh, stale: jnp.where(flag, fresh, stale), moved, kept)


def on_device(coeffs, p_slots, p_count, s_blocks, s_slots, s_count, q_slots, q_count):
    rows_n = lax.axis_size("row")
    cols_n = lax.axis_size("col")
    row_at = lax.axis_index("row")
    col_at = lax.axis_index("col")
    panel_rows, orbitals = coeffs.shape
    tile_rows = panel_rows // 128
    tile_cols = panel_rows * rows_n // cols_n // 128
    sub_span = cols_n // rows_n
    source = from_root(coeffs, "row", col_at // sub_span)
    column_rows = lax.dynamic_slice_in_dim(
        source, col_at % sub_span * (tile_cols * 128), tile_cols * 128, 0
    )
    slot_ids = p_slots[0, 0]
    p_max = slot_ids.shape[0]
    p_live = jnp.arange(p_max, dtype=jnp.int32) < p_count[0, 0]
    left = coeffs.reshape(tile_rows, 128, orbitals)[slot_ids // tile_cols]
    right = column_rows.reshape(tile_cols, 128, orbitals)[slot_ids % tile_cols]
    raw = jnp.einsum("pak,pbk->pab", left, right, preferred_element_type=jnp.float32)
    dense_blocks = jnp.where(p_live[:, None, None], raw, jnp.zeros_like(raw)).astype(jnp.bfloat16)
    p_code = jnp.where(p_live, slot_ids, -1)
    s_ids = s_slots[0, 0]
    s_max = s_ids.shape[0]
    s_live = jnp.arange(s_max, dtype=jnp.int32) < s_count[0, 0]
    s_code = jnp.where(s_live, s_ids, -1)
    s_local = s_blocks[0, 0]
    q_ids = q_slots[0, 0]
    q_max = q_ids.shape[0]
    q_live = jnp.arange(q_max, dtype=jnp.int32) < q_count[0, 0]
    q_row = q_ids // tile_cols
    q_col = q_ids % tile_cols
    zeros_out = jnp.zeros((q_max, 128, 128), jnp.float32)
    p_data = (dense_blocks, p_code)
    s_data = (s_local, s_code)
    level_count = rows_n.bit_length() - 1
    for level in range(level_count):
        moved = jax.tree.map(
            lambda part, own: part.astype(own.dtype),
            shifted(shortened(p_data), "col", -(1 << level)),
            p_data,
        )
        p_data = pick_tree(row_at >> level & 1 == 1, moved, p_data)
    row_offset = col_at % rows_n
    for level in range(level_count):
        moved = jax.tree.map(
            lambda part, own: part.astype(own.dtype),
            shifted(shortened(s_data), "row", -(1 << level)),
            s_data,
        )
        s_data = pick_tree(row_offset >> level & 1 == 1, moved, s_data)

    def advance(step_at, carry):
        summed, p_held, s_held = carry
        panel_at = (row_at + col_at + step_at) % cols_n
        summed = step_product(summed, p_held, s_held, panel_at // rows_n, q_row, q_col, tile_cols)
        p_held = jax.tree.map(
            lambda part, own: part.astype(own.dtype), shifted(shortened(p_held), "col", -1), p_held
        )
        s_held = jax.tree.map(
            lambda part, own: part.astype(own.dtype), shifted(shortened(s_held), "row", -1), s_held
        )
        return (summed, p_held, s_held)

    summed, p_data, s_data = lax.fori_loop(0, cols_n - 1, advance, (zeros_out, p_data, s_data))
    panel_at = (row_at + col_at + cols_n - 1) % cols_n
    summed = step_product(summed, p_data, s_data, panel_at // rows_n, q_row, q_col, tile_cols)
    product = jnp.where(q_live[:, None, None], summed, jnp.zeros_like(summed))
    return (dense_blocks.reshape(1, 1, p_max, 128, 128), product.reshape(1, 1, q_max, 128, 128))


def solution(mesh):
    return jax.shard_map(
        on_device,
        mesh=mesh,
        in_specs=(
            P("row", None),
            P("row", "col", None),
            P("row", "col"),
            P("row", "col", None, None, None),
            P("row", "col", None),
            P("row", "col"),
            P("row", "col", None),
            P("row", "col"),
        ),
        out_specs=(P("row", "col", None, None, None), P("row", "col", None, None, None)),
        check_vma=False,
    )
```

profile of v0, /device:TPU:0, one launch (start us, length us, event | category | flops | bytes accessed | tf_op | source)
XLA Modules:
  0.0 1880.5 jit_solution(13841358631608636264)
XLA Ops:
  7.2 13.8 broadcast_select_fusion
  22.6 2.7 copy.34
  26.0 19.3 %gather_fusion = bf16[64,128,2048]{2,1,0:T(8,128)(2,1)} fusion(bf16[32,128,2048]{2,1,0:T(8,128)(2,1)} %bitcast.130, s32[1024]{0:T(1024)S(1)} %get-tuple-element.386), kind=kCustom, calls=%fused_computation | custom fusion | bytes 67109120 | tf_op jit(solution)/shard_map/gather | solution.py:77
  45.3 329.8 %all-reduce.2.cloned.1.call-done = bf16[4096,2048]{1,0:T(8,128)(2,1)} async-done(((bf16[4096,2048]{1,0:T(8,128)(2,1)}), bf16[4096,2048]{1,0:T(8,128)(2,1)}) %all-reduce.2.cloned.1.call-update) | async-done | bytes 16777232 | tf_op jit(solution)/shard_map/psum | solution.py:9
  375.1 8.3 constant_dynamic-slice_fusion
  383.4 15.9 gather_fusion.1
  399.3 24.5 %select_convert_fusion = bf16[64,128,128]{2,1,0:T(8,128)(2,1)} fusion(pred[64]{0:T(512)(128)(4,1)S(1)} %iota_compare_fusion.5, bf16[64,128,2048]{2,1,0:T(8,128)(2,1)} %gather_fusion, bf16[64,128,2048]{2,1,0:T(8,128)(2,1)} %gather_fusion.1), kind=kOutput, calls=%fused_computation.45 | convolution fusion | flops 4297064448 | bytes 69206080 | tf_op jit(solution)/shard_map/pak,pbk->pab/dot_general | solution.py:79
  423.8 2.7 collective-permute-start.4
  426.5 3.1 broadcast_select_fusion.1
  431.3 19.1 %collective-permute-done.4 = bf16[64,128,128]{2,1,0:T(8,128)(2,1)} collective-permute-done((bf16[64,128,128]{2,1,0:T(8,128)(2,1)}, bf16[64,128,128]{2,1,0:T(8,128)(2,1)}, u32[]{:S(2)}, u32[]{:S(2)}) %collective-permute-start.4) | collective-permute-done | bytes 2097184 | tf_op jit(solution)/shard_map/ppermute | solution.py:23
  450.4 3.1 broadcast_select_fusion.3
  454.2 3.1 collective-permute-start.6
  457.9 2.4 collective-permute-start.10
  462.1 35.9 %collective-permute-done.6 = s32[64]{0:T(128)S(1)} collective-permute-done((s32[64]{0:T(128)S(1)}, s32[64]{0:T(128)S(1)}, u32[]{:S(2)}, u32[]{:S(2)}) %collective-permute-start.6) | collective-permute-done | bytes 288 | tf_op jit(solution)/shard_map/ppermute | solution.py:23
  504.0 1.8 broadcast_select_fusion.4
  505.9 2.7 copy.15
  508.5 1178.6 %while.25 = (s32[]{:T(128)}, f32[64,128,128]{2,1,0:T(8,128)}, bf16[64,128,128]{2,0,1:T(8,128)(2,1)}, s32[64]{0:T(128)S(1)}, bf16[64,128,128]{2,0,1:T(8,128)(2,1)...) while((s32[]{:T(128)}, f32[64,128,128]{2,1,0:T(8,128)}, ...), condition=%wide.region_2.3_spmd.clone, body=%wide.region_1.2_spmd.clone.sunk | while | flops 8625731584 | bytes 239103024 | solution.py:124
  510.3 5.4 collective-permute-start
  515.7 3.1 copy.48
  518.8 2.6 collective-permute-start.2
  522.3 13.8 convert_bitcast_fusion.4
  536.1 49.3 %reshape.448 = bf16[64,128,2048]{2,1,0:T(8,128)(2,1)} reshape(bf16[64,128,16,128]{3,2,1,0:T(8,128)(2,1)} %convert_bitcast_fusion.4) | data formatting | bytes 67108864 | tf_op jit(solution)/shard_map/while/body/eval_jaxpr/reshape | solution.py:38
  585.4 15.5 convolution_convert_fusion.2
  601.0 79.3 %select_add_fusion.2 = f32[64,128,128]{2,1,0:T(8,128)} fusion(f32[64,128,128]{2,1,0:T(8,128)} %get-tuple-element.471, pred[]{:T(512)S(6)} %compare.95, bf16[64,128,2048]{2,1,0:T(8,128)(2,1)} %reshape.448, bf16[2048,64,128]{2,1,0:T(8,128)(2,1)} %bitcast.128), kind=kOutput, calls=%fused_computation.6.clone.1 | convolution fusion | flops 4297064448 | bytes 75497472 | tf_op jit(solution)/shard_map/while/body/eval_jaxpr/qak,kqb->qab/dot_general | solution.py:52
  681.9 3.1 copy.48
  686.9 13.8 convert_bitcast_fusion.4
  700.7 49.3 %reshape.448 = bf16[64,128,2048]{2,1,0:T(8,128)(2,1)} reshape(bf16[64,128,16,128]{3,2,1,0:T(8,128)(2,1)} %convert_bitcast_fusion.4) | data formatting | bytes 67108864 | tf_op jit(solution)/shard_map/while/body/eval_jaxpr/reshape | solution.py:38
  750.0 15.5 convolution_convert_fusion.2
  765.6 80.5 %select_add_fusion.2 = f32[64,128,128]{2,1,0:T(8,128)} fusion(f32[64,128,128]{2,1,0:T(8,128)} %get-tuple-element.471, pred[]{:T(512)S(6)} %compare.95, bf16[64,128,2048]{2,1,0:T(8,128)(2,1)} %reshape.448, bf16[2048,64,128]{2,1,0:T(8,128)(2,1)} %bitcast.128), kind=kOutput, calls=%fused_computation.6.clone.1 | convolution fusion | flops 4297064448 | bytes 75497472 | tf_op jit(solution)/shard_map/while/body/eval_jaxpr/qak,kqb->qab/dot_general | solution.py:52
  849.3 3.1 copy.48
  852.4 2.5 collective-permute-start.2
  855.7 13.8 convert_bitcast_fusion.4
  869.6 49.3 %reshape.448 = bf16[64,128,2048]{2,1,0:T(8,128)(2,1)} reshape(bf16[64,128,16,128]{3,2,1,0:T(8,128)(2,1)} %convert_bitcast_fusion.4) | data formatting | bytes 67108864 | tf_op jit(solution)/shard_map/while/body/eval_jaxpr/reshape | solution.py:38
  918.9 15.5 convolution_convert_fusion.2
  934.4 80.5 %select_add_fusion.2 = f32[64,128,128]{2,1,0:T(8,128)} fusion(f32[64,128,128]{2,1,0:T(8,128)} %get-tuple-element.471, pred[]{:T(512)S(6)} %compare.95, bf16[64,128,2048]{2,1,0:T(8,128)(2,1)} %reshape.448, bf16[2048,64,128]{2,1,0:T(8,128)(2,1)} %bitcast.128), kind=kOutput, calls=%fused_computation.6.clone.1 | convolution fusion | flops 4297064448 | bytes 75497472 | tf_op jit(solution)/shard_map/while/body/eval_jaxpr/qak,kqb->qab/dot_general | solution.py:52
  1016.8 3.1 copy.48
  1021.8 13.8 convert_bitcast_fusion.4
  1035.7 49.3 %reshape.448 = bf16[64,128,2048]{2,1,0:T(8,128)(2,1)} reshape(bf16[64,128,16,128]{3,2,1,0:T(8,128)(2,1)} %convert_bitcast_fusion.4) | data formatting | bytes 67108864 | tf_op jit(solution)/shard_map/while/body/eval_jaxpr/reshape | solution.py:38
  1085.0 15.5 convolution_convert_fusion.2
  1100.5 80.5 %select_add_fusion.2 = f32[64,128,128]{2,1,0:T(8,128)} fusion(f32[64,128,128]{2,1,0:T(8,128)} %get-tuple-element.471, pred[]{:T(512)S(6)} %compare.95, bf16[64,128,2048]{2,1,0:T(8,128)(2,1)} %reshape.448, bf16[2048,64,128]{2,1,0:T(8,128)(2,1)} %bitcast.128), kind=kOutput, calls=%fused_computation.6.clone.1 | convolution fusion | flops 4297064448 | bytes 75497472 | tf_op jit(solution)/shard_map/while/body/eval_jaxpr/qak,kqb->qab/dot_general | solution.py:52
  1184.0 2.3 collective-permute-start.1
  1186.3 3.1 copy.48
  1189.4 2.6 collective-permute-start.2
  1192.9 13.8 convert_bitcast_fusion.4
  1206.8 49.3 %reshape.448 = bf16[64,128,2048]{2,1,0:T(8,128)(2,1)} reshape(bf16[64,128,16,128]{3,2,1,0:T(8,128)(2,1)} %convert_bitcast_fusion.4) | data formatting | bytes 67108864 | tf_op jit(solution)/shard_map/while/body/eval_jaxpr/reshape | solution.py:38
  1256.0 15.5 convolution_convert_fusion.2
  1271.6 80.5 %select_add_fusion.2 = f32[64,128,128]{2,1,0:T(8,128)} fusion(f32[64,128,128]{2,1,0:T(8,128)} %get-tuple-element.471, pred[]{:T(512)S(6)} %compare.95, bf16[64,128,2048]{2,1,0:T(8,128)(2,1)} %reshape.448, bf16[2048,64,128]{2,1,0:T(8,128)(2,1)} %bitcast.128), kind=kOutput, calls=%fused_computation.6.clone.1 | convolution fusion | flops 4297064448 | bytes 75497472 | tf_op jit(solution)/shard_map/while/body/eval_jaxpr/qak,kqb->qab/dot_general | solution.py:52
  1353.7 3.1 copy.48
  1358.7 13.8 convert_bitcast_fusion.4
  1372.6 49.3 %reshape.448 = bf16[64,128,2048]{2,1,0:T(8,128)(2,1)} reshape(bf16[64,128,16,128]{3,2,1,0:T(8,128)(2,1)} %convert_bitcast_fusion.4) | data formatting | bytes 67108864 | tf_op jit(solution)/shard_map/while/body/eval_jaxpr/reshape | solution.py:38
  1421.9 15.5 convolution_convert_fusion.2
  1437.4 80.5 %select_add_fusion.2 = f32[64,128,128]{2,1,0:T(8,128)} fusion(f32[64,128,128]{2,1,0:T(8,128)} %get-tuple-element.471, pred[]{:T(512)S(6)} %compare.95, bf16[64,128,2048]{2,1,0:T(8,128)(2,1)} %reshape.448, bf16[2048,64,128]{2,1,0:T(8,128)(2,1)} %bitcast.128), kind=kOutput, calls=%fused_computation.6.clone.1 | convolution fusion | flops 4297064448 | bytes 75497472 | tf_op jit(solution)/shard_map/while/body/eval_jaxpr/qak,kqb->qab/dot_general | solution.py:52
  1521.1 3.1 copy.48
  1524.2 2.5 collective-permute-start.2
  1527.6 13.8 convert_bitcast_fusion.4
  1541.4 49.3 %reshape.448 = bf16[64,128,2048]{2,1,0:T(8,128)(2,1)} reshape(bf16[64,128,16,128]{3,2,1,0:T(8,128)(2,1)} %convert_bitcast_fusion.4) | data formatting | bytes 67108864 | tf_op jit(solution)/shard_map/while/body/eval_jaxpr/reshape | solution.py:38
  1590.7 15.5 convolution_convert_fusion.2
  1606.2 80.5 %select_add_fusion.2 = f32[64,128,128]{2,1,0:T(8,128)} fusion(f32[64,128,128]{2,1,0:T(8,128)} %get-tuple-element.471, pred[]{:T(512)S(6)} %compare.95, bf16[64,128,2048]{2,1,0:T(8,128)(2,1)} %reshape.448, bf16[2048,64,128]{2,1,0:T(8,128)(2,1)} %bitcast.128), kind=kOutput, calls=%fused_computation.6.clone.1 | convolution fusion | flops 4297064448 | bytes 75497472 | tf_op jit(solution)/shard_map/while/body/eval_jaxpr/qak,kqb->qab/dot_general | solution.py:52
  1687.3 15.6 convert_bitcast_fusion.2
  1702.8 47.4 %copy.16 = bf16[64,128,16,128]{1,3,2,0:T(8,128)(2,1)} copy(bf16[64,128,16,128]{3,0,2,1:T(8,128)(2,1)} %convert_bitcast_fusion.2) | data formatting | bytes 67108864 | tf_op jit(solution)/shard_map/convert_element_type | solution.py:38
  1750.4 15.6 convert_bitcast_fusion.1
  1766.0 23.1 %copy.17 = bf16[16,128,64,128]{3,2,1,0:T(8,128)(2,1)} copy(bf16[16,128,64,128]{3,2,0,1:T(8,128)(2,1)} %convert_bitcast_fusion.1) | data formatting | bytes 67108864 | tf_op jit(solution)/shard_map/convert_element_type | solution.py:51
  1789.1 78.4 %fusion.14 = f32[64,128,128]{2,1,0:T(8,128)} fusion(bf16[64,128,2048]{1,2,0:T(8,128)(2,1)} %bitcast.131, bf16[2048,64,128]{2,1,0:T(8,128)(2,1)} %bitcast.132), kind=kOutput, calls=%fused_computation.39 | convolution fusion | flops 4294967296 | bytes 71303168 | tf_op jit(solution)/shard_map/qak,kqb->qab/dot_general | solution.py:52
  1867.5 5.9 select_bitcast_fusion
  (159 shorter events, 35.8 us)
Async XLA Ops:
  7.2 367.9 %all-reduce.2.cloned.1.call-start = ((), (), s32[]{:S(2)}) async-start(), calls=%async_computation | async-start | bytes 33554432 | tf_op jit(solution)/shard_map/psum | solution.py:9
  21.0 1.6 copy-start
  22.6 3.3 copy-start.2
  25.3 401.2 %collective-permute-start.8 = (bf16[64,128,128]{2,0,1:T(8,128)(2,1)}, bf16[64,128,128]{2,0,1:T(8,128)(2,1)}, u32[]{:S(2)}, u32[]{:S(2)}) collective-permute-start(bf16[64,128,128]{2,0,1:T(8,128)(2,1)} %bitcast.107), channel_id=1, source_target_pairs={{8,0},{16,8},{24,16},{0,24},{9,1},{17,9},{25,17},{1,25},{10,2},{18... | collective-permute-start | bytes 6291464 | tf_op jit(solution)/shard_map/ppermute | solution.py:23
  423.8 26.5 %collective-permute-start.4 = (bf16[64,128,128]{2,1,0:T(8,128)(2,1)}, bf16[64,128,128]{2,1,0:T(8,128)(2,1)}, u32[]{:S(2)}, u32[]{:S(2)}) collective-permute-start(bf16[64,128,128]{2,1,0:T(8,128)(2,1)} %select_convert_fusion), channel_id=1, source_target_pairs={{1,0},{2,1},{3,2},{4,3},{5,4},{6,5},{7,6},{0,7},{9,8},{10,9},{11,1... | collective-permute-start | bytes 6291464 | tf_op jit(solution)/shard_map/ppermute | solution.py:23
  429.6 28.3 %copy-start.3 = (s32[1,1,64]{2,1,0:T(1,128)S(1)}, s32[1,1,64]{2,1,0:T(1,128)}, u32[]{:S(2)}) copy-start(s32[1,1,64]{2,1,0:T(1,128)} %param.14) | copy-start | bytes 772
  429.6 31.9 %copy-start.5 = (s32[1,1,64]{2,1,0:T(1,128)S(1)}, s32[1,1,64]{2,1,0:T(1,128)}, u32[]{:S(2)}) copy-start(s32[1,1,64]{2,1,0:T(1,128)} %param.16) | copy-start | bytes 772
  429.7 72.8 %collective-permute-start.9 = (bf16[64,128,128]{2,0,1:T(8,128)(2,1)S(1)}, bf16[64,128,128]{2,0,1:T(8,128)(2,1)}, u32[]{:S(2)}, u32[]{:S(2)}) collective-permute-start(bf16[64,128,128]{2,0,1:T(8,128)(2,1)S(1)} %broadcast_select_fusion.1), channel_id=1, source_target_pairs={{16,0},{24,8},{0,16},{8,24},{17,1},{25,9},{1,17},{9,25},{18,2},{26... | collective-permute-start | bytes 6291464 | tf_op jit(solution)/shard_map/ppermute | solution.py:23
  453.5 50.5 %collective-permute-start.5 = (bf16[64,128,128]{2,1,0:T(8,128)(2,1)}, bf16[64,128,128]{2,1,0:T(8,128)(2,1)}, u32[]{:S(2)}, u32[]{:S(2)}) collective-permute-start(bf16[64,128,128]{2,1,0:T(8,128)(2,1)} %broadcast_select_fusion.3), channel_id=1, source_target_pairs={{2,0},{3,1},{4,2},{5,3},{6,4},{7,5},{0,6},{1,7},{10,8},{11,9},{12,... | collective-permute-start | bytes 6291464 | tf_op jit(solution)/shard_map/ppermute | solution.py:23
  454.2 43.9 %collective-permute-start.6 = (s32[64]{0:T(128)S(1)}, s32[64]{0:T(128)S(1)}, u32[]{:S(2)}, u32[]{:S(2)}) collective-permute-start(s32[64]{0:T(128)S(1)} %bitcast_select_fusion), channel_id=1, source_target_pairs={{1,0},{2,1},{3,2},{4,3},{5,4},{6,5},{7,6},{0,7},{9,8},{10,9},{11,1... | collective-permute-start | bytes 776 | tf_op jit(solution)/shard_map/ppermute | solution.py:23
  457.9 40.9 %collective-permute-start.10 = (s32[64]{0:T(128)S(1)}, s32[64]{0:T(128)S(1)}, u32[]{:S(2)}, u32[]{:S(2)}) collective-permute-start(s32[64]{0:T(128)S(1)} %compare_select_fusion.15), channel_id=1, source_target_pairs={{8,0},{16,8},{24,16},{0,24},{9,1},{17,9},{25,17},{1,25},{10,2},{18... | collective-permute-start | bytes 776 | tf_op jit(solution)/shard_map/ppermute | solution.py:23
  498.0 3.8 collective-permute-start.7
  498.9 3.6 collective-permute-start.11
  510.3 170.0 %collective-permute-start = (bf16[64,128,128]{2,0,1:T(8,128)(2,1)S(1)}, bf16[64,128,128]{2,0,1:T(8,128)(2,1)}, u32[]{:S(2)}, u32[]{:S(2)}) collective-permute-start(bf16[64,128,128]{2,0,1:T(8,128)(2,1)S(1)} %copy.46), channel_id=1, source_target_pairs={{1,0},{2,1},{3,2},{4,3},{5,4},{6,5},{7,6},{0,7},{9,8},{10,9},{11,1... | collective-permute-start | bytes 6291464 | tf_op jit(solution)/shard_map/while/body/eval_jaxpr/ppermute | solution.py:23
  515.6 164.6 %collective-permute-start.1 = (s32[64]{0:T(128)S(1)}, s32[64]{0:T(128)S(1)}, u32[]{:S(2)}, u32[]{:S(2)}) collective-permute-start(s32[64]{0:T(128)S(1)} %copy.47), channel_id=1, source_target_pairs={{1,0},{2,1},{3,2},{4,3},{5,4},{6,5},{7,6},{0,7},{9,8},{10,9},{11,1... | collective-permute-start | bytes 776 | tf_op jit(solution)/shard_map/while/body/eval_jaxpr/ppermute | solution.py:23
  518.8 161.5 %collective-permute-start.2 = (bf16[64,128,128]{2,0,1:T(8,128)(2,1)}, bf16[64,128,128]{2,0,1:T(8,128)(2,1)}, u32[]{:S(2)}, u32[]{:S(2)}) collective-permute-start(bf16[64,128,128]{2,0,1:T(8,128)(2,1)} %copy.48), channel_id=1, source_target_pairs={{8,0},{16,8},{24,16},{0,24},{9,1},{17,9},{25,17},{1,25},{10,2},{18... | collective-permute-start | bytes 6291464 | tf_op jit(solution)/shard_map/while/body/eval_jaxpr/ppermute | solution.py:23
  521.4 158.8 %collective-permute-start.3 = (s32[64]{0:T(128)S(1)}, s32[64]{0:T(128)S(1)}, u32[]{:S(2)}, u32[]{:S(2)}) collective-permute-start(s32[64]{0:T(128)S(1)} %copy.49), channel_id=1, source_target_pairs={{8,0},{16,8},{24,16},{0,24},{9,1},{17,9},{25,17},{1,25},{10,2},{18... | collective-permute-start | bytes 776 | tf_op jit(solution)/shard_map/while/body/eval_jaxpr/ppermute | solution.py:23
  681.9 164.2 %collective-permute-start = (bf16[64,128,128]{2,0,1:T(8,128)(2,1)S(1)}, bf16[64,128,128]{2,0,1:T(8,128)(2,1)}, u32[]{:S(2)}, u32[]{:S(2)}) collective-permute-start(bf16[64,128,128]{2,0,1:T(8,128)(2,1)S(1)} %copy.46), channel_id=1, source_target_pairs={{1,0},{2,1},{3,2},{4,3},{5,4},{6,5},{7,6},{0,7},{9,8},{10,9},{11,1... | collective-permute-start | bytes 6291464 | tf_op jit(solution)/shard_map/while/body/eval_jaxpr/ppermute | solution.py:23
  681.9 164.2 %collective-permute-start.1 = (s32[64]{0:T(128)S(1)}, s32[64]{0:T(128)S(1)}, u32[]{:S(2)}, u32[]{:S(2)}) collective-permute-start(s32[64]{0:T(128)S(1)} %copy.47), channel_id=1, source_target_pairs={{1,0},{2,1},{3,2},{4,3},{5,4},{6,5},{7,6},{0,7},{9,8},{10,9},{11,1... | collective-permute-start | bytes 776 | tf_op jit(solution)/shard_map/while/body/eval_jaxpr/ppermute | solution.py:23
  685.0 161.1 %collective-permute-start.2 = (bf16[64,128,128]{2,0,1:T(8,128)(2,1)}, bf16[64,128,128]{2,0,1:T(8,128)(2,1)}, u32[]{:S(2)}, u32[]{:S(2)}) collective-permute-start(bf16[64,128,128]{2,0,1:T(8,128)(2,1)} %copy.48), channel_id=1, source_target_pairs={{8,0},{16,8},{24,16},{0,24},{9,1},{17,9},{25,17},{1,25},{10,2},{18... | collective-permute-start | bytes 6291464 | tf_op jit(solution)/shard_map/while/body/eval_jaxpr/ppermute | solution.py:23
  686.2 159.9 %collective-permute-start.3 = (s32[64]{0:T(128)S(1)}, s32[64]{0:T(128)S(1)}, u32[]{:S(2)}, u32[]{:S(2)}) collective-permute-start(s32[64]{0:T(128)S(1)} %copy.49), channel_id=1, source_target_pairs={{8,0},{16,8},{24,16},{0,24},{9,1},{17,9},{25,17},{1,25},{10,2},{18... | collective-permute-start | bytes 776 | tf_op jit(solution)/shard_map/while/body/eval_jaxpr/ppermute | solution.py:23
  847.7 167.2 %collective-permute-start = (bf16[64,128,128]{2,0,1:T(8,128)(2,1)S(1)}, bf16[64,128,128]{2,0,1:T(8,128)(2,1)}, u32[]{:S(2)}, u32[]{:S(2)}) collective-permute-start(bf16[64,128,128]{2,0,1:T(8,128)(2,1)S(1)} %copy.46), channel_id=1, source_target_pairs={{1,0},{2,1},{3,2},{4,3},{5,4},{6,5},{7,6},{0,7},{9,8},{10,9},{11,1... | collective-permute-start | bytes 6291464 | tf_op jit(solution)/shard_map/while/body/eval_jaxpr/ppermute | solution.py:23
  848.1 166.8 %collective-permute-start.1 = (s32[64]{0:T(128)S(1)}, s32[64]{0:T(128)S(1)}, u32[]{:S(2)}, u32[]{:S(2)}) collective-permute-start(s32[64]{0:T(128)S(1)} %copy.47), channel_id=1, source_target_pairs={{1,0},{2,1},{3,2},{4,3},{5,4},{6,5},{7,6},{0,7},{9,8},{10,9},{11,1... | collective-permute-start | bytes 776 | tf_op jit(solution)/shard_map/while/body/eval_jaxpr/ppermute | solution.py:23
  852.4 162.5 %collective-permute-start.2 = (bf16[64,128,128]{2,0,1:T(8,128)(2,1)}, bf16[64,128,128]{2,0,1:T(8,128)(2,1)}, u32[]{:S(2)}, u32[]{:S(2)}) collective-permute-start(bf16[64,128,128]{2,0,1:T(8,128)(2,1)} %copy.48), channel_id=1, source_target_pairs={{8,0},{16,8},{24,16},{0,24},{9,1},{17,9},{25,17},{1,25},{10,2},{18... | collective-permute-start | bytes 6291464 | tf_op jit(solution)/shard_map/while/body/eval_jaxpr/ppermute | solution.py:23
  854.9 160.0 %collective-permute-start.3 = (s32[64]{0:T(128)S(1)}, s32[64]{0:T(128)S(1)}, u32[]{:S(2)}, u32[]{:S(2)}) collective-permute-start(s32[64]{0:T(128)S(1)} %copy.49), channel_id=1, source_target_pairs={{8,0},{16,8},{24,16},{0,24},{9,1},{17,9},{25,17},{1,25},{10,2},{18... | collective-permute-start | bytes 776 | tf_op jit(solution)/shard_map/while/body/eval_jaxpr/ppermute | solution.py:23
  1016.5 164.5 %collective-permute-start = (bf16[64,128,128]{2,0,1:T(8,128)(2,1)S(1)}, bf16[64,128,128]{2,0,1:T(8,128)(2,1)}, u32[]{:S(2)}, u32[]{:S(2)}) collective-permute-start(bf16[64,128,128]{2,0,1:T(8,128)(2,1)S(1)} %copy.46), channel_id=1, source_target_pairs={{1,0},{2,1},{3,2},{4,3},{5,4},{6,5},{7,6},{0,7},{9,8},{10,9},{11,1... | collective-permute-start | bytes 6291464 | tf_op jit(solution)/shard_map/while/body/eval_jaxpr/ppermute | solution.py:23
  1016.5 164.5 %collective-permute-start.1 = (s32[64]{0:T(128)S(1)}, s32[64]{0:T(128)S(1)}, u32[]{:S(2)}, u32[]{:S(2)}) collective-permute-start(s32[64]{0:T(128)S(1)} %copy.47), channel_id=1, source_target_pairs={{1,0},{2,1},{3,2},{4,3},{5,4},{6,5},{7,6},{0,7},{9,8},{10,9},{11,1... | collective-permute-start | bytes 776 | tf_op jit(solution)/shard_map/while/body/eval_jaxpr/ppermute | solution.py:23
  1019.9 161.1 %collective-permute-start.2 = (bf16[64,128,128]{2,0,1:T(8,128)(2,1)}, bf16[64,128,128]{2,0,1:T(8,128)(2,1)}, u32[]{:S(2)}, u32[]{:S(2)}) collective-permute-start(bf16[64,128,128]{2,0,1:T(8,128)(2,1)} %copy.48), channel_id=1, source_target_pairs={{8,0},{16,8},{24,16},{0,24},{9,1},{17,9},{25,17},{1,25},{10,2},{18... | collective-permute-start | bytes 6291464 | tf_op jit(solution)/shard_map/while/body/eval_jaxpr/ppermute | solution.py:23
  1021.1 159.9 %collective-permute-start.3 = (s32[64]{0:T(128)S(1)}, s32[64]{0:T(128)S(1)}, u32[]{:S(2)}, u32[]{:S(2)}) collective-permute-start(s32[64]{0:T(128)S(1)} %copy.49), channel_id=1, source_target_pairs={{8,0},{16,8},{24,16},{0,24},{9,1},{17,9},{25,17},{1,25},{10,2},{18... | collective-permute-start | bytes 776 | tf_op jit(solution)/shard_map/while/body/eval_jaxpr/ppermute | solution.py:23
  1182.6 169.5 %collective-permute-start = (bf16[64,128,128]{2,0,1:T(8,128)(2,1)S(1)}, bf16[64,128,128]{2,0,1:T(8,128)(2,1)}, u32[]{:S(2)}, u32[]{:S(2)}) collective-permute-start(bf16[64,128,128]{2,0,1:T(8,128)(2,1)S(1)} %copy.46), channel_id=1, source_target_pairs={{1,0},{2,1},{3,2},{4,3},{5,4},{6,5},{7,6},{0,7},{9,8},{10,9},{11,1... | collective-permute-start | bytes 6291464 | tf_op jit(solution)/shard_map/while/body/eval_jaxpr/ppermute | solution.py:23
  1184.0 168.1 %collective-permute-start.1 = (s32[64]{0:T(128)S(1)}, s32[64]{0:T(128)S(1)}, u32[]{:S(2)}, u32[]{:S(2)}) collective-permute-start(s32[64]{0:T(128)S(1)} %copy.47), channel_id=1, source_target_pairs={{1,0},{2,1},{3,2},{4,3},{5,4},{6,5},{7,6},{0,7},{9,8},{10,9},{11,1... | collective-permute-start | bytes 776 | tf_op jit(solution)/shard_map/while/body/eval_jaxpr/ppermute | solution.py:23
  1189.4 162.7 %collective-permute-start.2 = (bf16[64,128,128]{2,0,1:T(8,128)(2,1)}, bf16[64,128,128]{2,0,1:T(8,128)(2,1)}, u32[]{:S(2)}, u32[]{:S(2)}) collective-permute-start(bf16[64,128,128]{2,0,1:T(8,128)(2,1)} %copy.48), channel_id=1, source_target_pairs={{8,0},{16,8},{24,16},{0,24},{9,1},{17,9},{25,17},{1,25},{10,2},{18... | collective-permute-start | bytes 6291464 | tf_op jit(solution)/shard_map/while/body/eval_jaxpr/ppermute | solution.py:23
  1192.1 160.0 %collective-permute-start.3 = (s32[64]{0:T(128)S(1)}, s32[64]{0:T(128)S(1)}, u32[]{:S(2)}, u32[]{:S(2)}) collective-permute-start(s32[64]{0:T(128)S(1)} %copy.49), channel_id=1, source_target_pairs={{8,0},{16,8},{24,16},{0,24},{9,1},{17,9},{25,17},{1,25},{10,2},{18... | collective-permute-start | bytes 776 | tf_op jit(solution)/shard_map/while/body/eval_jaxpr/ppermute | solution.py:23
  1353.7 164.2 %collective-permute-start = (bf16[64,128,128]{2,0,1:T(8,128)(2,1)S(1)}, bf16[64,128,128]{2,0,1:T(8,128)(2,1)}, u32[]{:S(2)}, u32[]{:S(2)}) collective-permute-start(bf16[64,128,128]{2,0,1:T(8,128)(2,1)S(1)} %copy.46), channel_id=1, source_target_pairs={{1,0},{2,1},{3,2},{4,3},{5,4},{6,5},{7,6},{0,7},{9,8},{10,9},{11,1... | collective-permute-start | bytes 6291464 | tf_op jit(solution)/shard_map/while/body/eval_jaxpr/ppermute | solution.py:23
  1353.7 164.2 %collective-permute-start.1 = (s32[64]{0:T(128)S(1)}, s32[64]{0:T(128)S(1)}, u32[]{:S(2)}, u32[]{:S(2)}) collective-permute-start(s32[64]{0:T(128)S(1)} %copy.47), channel_id=1, source_target_pairs={{1,0},{2,1},{3,2},{4,3},{5,4},{6,5},{7,6},{0,7},{9,8},{10,9},{11,1... | collective-permute-start | bytes 776 | tf_op jit(solution)/shard_map/while/body/eval_jaxpr/ppermute | solution.py:23
  1356.8 161.1 %collective-permute-start.2 = (bf16[64,128,128]{2,0,1:T(8,128)(2,1)}, bf16[64,128,128]{2,0,1:T(8,128)(2,1)}, u32[]{:S(2)}, u32[]{:S(2)}) collective-permute-start(bf16[64,128,128]{2,0,1:T(8,128)(2,1)} %copy.48), channel_id=1, source_target_pairs={{8,0},{16,8},{24,16},{0,24},{9,1},{17,9},{25,17},{1,25},{10,2},{18... | collective-permute-start | bytes 6291464 | tf_op jit(solution)/shard_map/while/body/eval_jaxpr/ppermute | solution.py:23
  1358.0 159.9 %collective-permute-start.3 = (s32[64]{0:T(128)S(1)}, s32[64]{0:T(128)S(1)}, u32[]{:S(2)}, u32[]{:S(2)}) collective-permute-start(s32[64]{0:T(128)S(1)} %copy.49), channel_id=1, source_target_pairs={{8,0},{16,8},{24,16},{0,24},{9,1},{17,9},{25,17},{1,25},{10,2},{18... | collective-permute-start | bytes 776 | tf_op jit(solution)/shard_map/while/body/eval_jaxpr/ppermute | solution.py:23
  1519.5 167.2 %collective-permute-start = (bf16[64,128,128]{2,0,1:T(8,128)(2,1)S(1)}, bf16[64,128,128]{2,0,1:T(8,128)(2,1)}, u32[]{:S(2)}, u32[]{:S(2)}) collective-permute-start(bf16[64,128,128]{2,0,1:T(8,128)(2,1)S(1)} %copy.46), channel_id=1, source_target_pairs={{1,0},{2,1},{3,2},{4,3},{5,4},{6,5},{7,6},{0,7},{9,8},{10,9},{11,1... | collective-permute-start | bytes 6291464 | tf_op jit(solution)/shard_map/while/body/eval_jaxpr/ppermute | solution.py:23
  1519.5 167.2 %collective-permute-start.1 = (s32[64]{0:T(128)S(1)}, s32[64]{0:T(128)S(1)}, u32[]{:S(2)}, u32[]{:S(2)}) collective-permute-start(s32[64]{0:T(128)S(1)} %copy.47), channel_id=1, source_target_pairs={{1,0},{2,1},{3,2},{4,3},{5,4},{6,5},{7,6},{0,7},{9,8},{10,9},{11,1... | collective-permute-start | bytes 776 | tf_op jit(solution)/shard_map/while/body/eval_jaxpr/ppermute | solution.py:23
  1524.2 162.5 %collective-permute-start.2 = (bf16[64,128,128]{2,0,1:T(8,128)(2,1)}, bf16[64,128,128]{2,0,1:T(8,128)(2,1)}, u32[]{:S(2)}, u32[]{:S(2)}) collective-permute-start(bf16[64,128,128]{2,0,1:T(8,128)(2,1)} %copy.48), channel_id=1, source_target_pairs={{8,0},{16,8},{24,16},{0,24},{9,1},{17,9},{25,17},{1,25},{10,2},{18... | collective-permute-start | bytes 6291464 | tf_op jit(solution)/shard_map/while/body/eval_jaxpr/ppermute | solution.py:23
  1526.7 160.0 %collective-permute-start.3 = (s32[64]{0:T(128)S(1)}, s32[64]{0:T(128)S(1)}, u32[]{:S(2)}, u32[]{:S(2)}) collective-permute-start(s32[64]{0:T(128)S(1)} %copy.49), channel_id=1, source_target_pairs={{8,0},{16,8},{24,16},{0,24},{9,1},{17,9},{25,17},{1,25},{10,2},{18... | collective-permute-start | bytes 776 | tf_op jit(solution)/shard_map/while/body/eval_jaxpr/ppermute | solution.py:23
  1702.8 47.5 %copy-start.4 = (s32[64]{0:T(128)S(1)}, s32[64]{0:T(128)}, u32[]{:S(2)}) copy-start(s32[64]{0:T(128)} %fusion.26) | copy-start | bytes 772
  1789.1 78.4 %copy-start.1 = (pred[64]{0:T(512)(128)(4,1)S(1)}, pred[64]{0:T(512)(128)(4,1)}, u32[]{:S(2)}) copy-start(pred[64]{0:T(512)(128)(4,1)} %iota_compare_fusion.4) | copy-start | bytes 196
Sparse Core Ops, SparseCore 0:
  21.1 353.9 all-reduce.1
where the time goes:
time: 1900 us; the launch traced here: 1880 us
  matrix products  902 us (47%)
  local copies, waits for them, and re-layouts  499 us (26%)
  waiting for transfers between devices  387 us (20%)
  starting transfers between devices  43.5 us (2%)
  other arithmetic  31.6 us (2%)
    dot_general x8, matrix products, step_product(): jnp.einsum('qak,kqb->qab', left_rows, right_cols, preferred_element_type=...  641 us
    reshape x7, local copies, waits for them, and re-layouts, step_product(): left_rows.astype(jnp.bfloat16).reshape(q_row.shape[0], 128, tile_cols * 128)  345 us
    psum x1, waiting for transfers between devices, from_root(): return lax.psum(block, axis)  330 us
    dot_general x8, matrix products, step_product(): jnp.einsum('skq,sab->kaqb', pick_right, s_blocks, preferred_element_type=...  124 us
    dot_general x8, matrix products, step_product(): jnp.einsum('pqk,pab->qakb', pick_left, p_blocks, preferred_element_type=j...  112 us
    ppermute x36, waiting for transfers between devices, shifted(): return lax.ppermute(block, axis, route)  56.9 us
    convert_element_type x1, local copies, waits for them, and re-layouts, step_product(): left_rows.astype(jnp.bfloat16).reshape(q_row.shape[0], 128, tile_cols * 128)  47.4 us
    ppermute x36, starting transfers between devices, shifted(): return lax.ppermute(block, axis, route)  43.4 us
  transfers between devices with their start and end apart: 37, of which 5 were waited for; matrix products, arithmetic and copies ran while one was open for 65% of the time, Pallas kernels for 0%

commit v1 on v0

--- a/solution.py
+++ b/solution.py
@@ -4,9 +4,15 @@
 from jax.sharding import PartitionSpec as P
 
 
+def summed_here(block, axis):
+    shards = lax.all_gather(block, axis, axis=0, tiled=False)
+    total = shards.sum(axis=0)
+    return total
+
+
 def from_root(block, axis, source):
     block = jnp.where(lax.axis_index(axis) == source, block, jnp.zeros_like(block))
-    return lax.psum(block, axis)
+    return summed_here(block, axis)
 
 
 def shortened(shard):

time: 1900 us -> 2180 us (1.15)
  waiting for transfers between devices: 387 us -> 626 us
  other arithmetic: 31.6 us -> 62 us
    all_gather x0 -> x1, waiting for transfers between devices: none -> 568 us  [summed_here(): shards = lax.all_gather(block, axis, axis=0, tiled=False)]
    psum x1 -> x0, waiting for transfers between devices: 330 us -> none  [from_root(): return lax.psum(block, axis)]
    reduce_sum x0 -> x1, other arithmetic: none -> 30.4 us  [summed_here(): total = shards.sum(axis=0)]
  transfers between devices with their start and end apart: 37 -> 37, of which waited for: 5 -> 4; matrix products, arithmetic and copies ran while one was open for 65% -> 58% of each run, Pallas kernels for 0% -> 0%
where the time goes in v1:
time: 2180 us; the launch traced here: 2160 us
  matrix products  902 us (41%)
  waiting for transfers between devices  626 us (29%)
  local copies, waits for them, and re-layouts  510 us (23%)
  other arithmetic  62 us (3%)
  starting transfers between devices  40.1 us (2%)
    dot_general x8, matrix products, step_product(): jnp.einsum('qak,kqb->qab', left_rows, right_cols, preferred_element_type=...  641 us
    all_gather x1, waiting for transfers between devices, summed_here(): shards = lax.all_gather(block, axis, axis=0, tiled=False)  568 us
    reshape x7, local copies, waits for them, and re-layouts, step_product(): left_rows.astype(jnp.bfloat16).reshape(q_row.shape[0], 128, tile_cols * 128)  345 us
    dot_general x8, matrix products, step_product(): jnp.einsum('skq,sab->kaqb', pick_right, s_blocks, preferred_element_type=...  124 us
    dot_general x8, matrix products, step_product(): jnp.einsum('pqk,pab->qakb', pick_left, p_blocks, preferred_element_type=j...  113 us
    ppermute x36, waiting for transfers between devices, shifted(): return lax.ppermute(block, axis, route)  57.9 us
    convert_element_type x1, local copies, waits for them, and re-layouts, step_product(): left_rows.astype(jnp.bfloat16).reshape(q_row.shape[0], 128, tile_cols * 128)  47.5 us
  transfers between devices with their start and end apart: 37, of which 4 were waited for; matrix products, arithmetic and copies ran while one was open for 58% of the time, Pallas kernels for 0%

profile of v1, /device:TPU:0, one launch (start us, length us, event | category | flops | bytes accessed | tf_op | source)
XLA Modules:
  0.0 2157.2 jit_solution(15117901549779162671)
XLA Ops:
  7.2 13.8 broadcast_select_fusion
  22.6 2.7 copy.34
  26.0 30.1 %gather_fusion = bf16[64,128,2048]{2,1,0:T(8,128)(2,1)} fusion(bf16[32,128,2048]{2,1,0:T(8,128)(2,1)} %bitcast.131, s32[1024]{0:T(1024)S(1)} %get-tuple-element.386), kind=kCustom, calls=%fused_computation | custom fusion | bytes 67109120 | tf_op jit(solution)/shard_map/gather | solution.py:83
  56.1 567.7 %all-gather.3.cloned.1.call-done = bf16[16384,2048]{1,0:T(8,128)(2,1)} async-done(((bf16[4096,2048]{1,0:T(8,128)(2,1)}), bf16[16384,2048]{1,0:T(8,128)(2,1)}) %all-gather.3.cloned.1.call-update) | async-done | bytes 67108880 | tf_op jit(solution)/shard_map/all_gather | solution.py:8
  623.8 30.4 %reduce_sum.12 = bf16[4096,2048]{1,0:T(8,128)(2,1)} reduce(bf16[4,4096,2048]{2,1,0:T(8,128)(2,1)} %bitcast.4, bf16[]{:T(256)} %constant.359.clone.1), dimensions={0}, to_apply=%region_0.1 | reduce | flops 25165824 | bytes 83886080 | tf_op jit(solution)/shard_map/reduce_sum | solution.py:9
  654.2 8.3 constant_dynamic-slice_fusion
  662.5 15.8 gather_fusion.1
  678.3 24.5 %select_convert_fusion = bf16[64,128,128]{2,1,0:T(8,128)(2,1)} fusion(pred[64]{0:T(512)(128)(4,1)S(1)} %iota_compare_fusion.5, bf16[64,128,2048]{2,1,0:T(8,128)(2,1)} %gather_fusion, bf16[64,128,2048]{2,1,0:T(8,128)(2,1)} %gather_fusion.1), kind=kOutput, calls=%fused_computation.45 | convolution fusion | flops 4297064448 | bytes 69206080 | tf_op jit(solution)/shard_map/pak,pbk->pab/dot_general | solution.py:85
  702.8 3.0 collective-permute-start.4
  706.5 3.1 broadcast_select_fusion.1
  711.2 18.5 collective-permute-done.4
  729.7 3.1 broadcast_select_fusion.3
  735.0 2.8 collective-permute-start.6
  741.1 36.3 %collective-permute-done.6 = s32[64]{0:T(128)S(1)} collective-permute-done((s32[64]{0:T(128)S(1)}, s32[64]{0:T(128)S(1)}, u32[]{:S(2)}, u32[]{:S(2)}) %collective-permute-start.6) | collective-permute-done | bytes 288 | tf_op jit(solution)/shard_map/ppermute | solution.py:29
  778.3 3.0 collective-permute-done.7
  782.8 1.8 broadcast_select_fusion.4
  784.6 2.7 copy.15
  787.2 1176.3 %while.25 = (s32[]{:T(128)}, f32[64,128,128]{2,1,0:T(8,128)}, bf16[64,128,128]{2,0,1:T(8,128)(2,1)}, s32[64]{0:T(128)S(1)}, bf16[64,128,128]{2,0,1:T(8,128)(2,1)...) while((s32[]{:T(128)}, f32[64,128,128]{2,1,0:T(8,128)}, ...), condition=%wide.region_2.3_spmd.clone, body=%wide.region_1.2_spmd.clone.sunk | while | flops 8625731584 | bytes 239103024 | solution.py:130
  789.0 6.0 collective-permute-start
  795.0 3.1 copy.47
  801.4 13.9 convert_bitcast_fusion.4
  815.2 49.3 %reshape.449 = bf16[64,128,2048]{2,1,0:T(8,128)(2,1)} reshape(bf16[64,128,16,128]{3,2,1,0:T(8,128)(2,1)} %convert_bitcast_fusion.4) | data formatting | bytes 67108864 | tf_op jit(solution)/shard_map/while/body/eval_jaxpr/reshape | solution.py:44
  864.5 15.5 convolution_convert_fusion.2
  880.0 79.3 %select_add_fusion.2 = f32[64,128,128]{2,1,0:T(8,128)} fusion(f32[64,128,128]{2,1,0:T(8,128)} %get-tuple-element.471, pred[]{:T(512)S(6)} %compare.95, bf16[64,128,2048]{2,1,0:T(8,128)(2,1)} %reshape.449, bf16[2048,64,128]{2,1,0:T(8,128)(2,1)} %bitcast.129), kind=kOutput, calls=%fused_computation.6.clone.1 | convolution fusion | flops 4297064448 | bytes 75497472 | tf_op jit(solution)/shard_map/while/body/eval_jaxpr/qak,kqb->qab/dot_general | solution.py:58
  959.4 1.6 copy.45
  961.0 3.1 copy.47
  966.1 13.8 convert_bitcast_fusion.4
  980.0 49.3 %reshape.449 = bf16[64,128,2048]{2,1,0:T(8,128)(2,1)} reshape(bf16[64,128,16,128]{3,2,1,0:T(8,128)(2,1)} %convert_bitcast_fusion.4) | data formatting | bytes 67108864 | tf_op jit(solution)/shard_map/while/body/eval_jaxpr/reshape | solution.py:44
  1029.3 15.5 convolution_convert_fusion.2
  1044.8 80.5 %select_add_fusion.2 = f32[64,128,128]{2,1,0:T(8,128)} fusion(f32[64,128,128]{2,1,0:T(8,128)} %get-tuple-element.471, pred[]{:T(512)S(6)} %compare.95, bf16[64,128,2048]{2,1,0:T(8,128)(2,1)} %reshape.449, bf16[2048,64,128]{2,1,0:T(8,128)(2,1)} %bitcast.129), kind=kOutput, calls=%fused_computation.6.clone.1 | convolution fusion | flops 4297064448 | bytes 75497472 | tf_op jit(solution)/shard_map/while/body/eval_jaxpr/qak,kqb->qab/dot_general | solution.py:58
  1125.4 1.6 copy.45
  1126.9 3.1 copy.47
  1133.3 13.8 convert_bitcast_fusion.4
  1147.2 49.3 %reshape.449 = bf16[64,128,2048]{2,1,0:T(8,128)(2,1)} reshape(bf16[64,128,16,128]{3,2,1,0:T(8,128)(2,1)} %convert_bitcast_fusion.4) | data formatting | bytes 67108864 | tf_op jit(solution)/shard_map/while/body/eval_jaxpr/reshape | solution.py:44
  1196.5 15.5 convolution_convert_fusion.2
  1212.0 80.5 %select_add_fusion.2 = f32[64,128,128]{2,1,0:T(8,128)} fusion(f32[64,128,128]{2,1,0:T(8,128)} %get-tuple-element.471, pred[]{:T(512)S(6)} %compare.95, bf16[64,128,2048]{2,1,0:T(8,128)(2,1)} %reshape.449, bf16[2048,64,128]{2,1,0:T(8,128)(2,1)} %bitcast.129), kind=kOutput, calls=%fused_computation.6.clone.1 | convolution fusion | flops 4297064448 | bytes 75497472 | tf_op jit(solution)/shard_map/while/body/eval_jaxpr/qak,kqb->qab/dot_general | solution.py:58
  1292.5 1.6 copy.45
  1294.1 3.1 copy.47
  1299.4 13.8 convert_bitcast_fusion.4
  1313.2 49.3 %reshape.449 = bf16[64,128,2048]{2,1,0:T(8,128)(2,1)} reshape(bf16[64,128,16,128]{3,2,1,0:T(8,128)(2,1)} %convert_bitcast_fusion.4) | data formatting | bytes 67108864 | tf_op jit(solution)/shard_map/while/body/eval_jaxpr/reshape | solution.py:44
  1362.5 15.5 convolution_convert_fusion.2
  1378.1 80.5 %select_add_fusion.2 = f32[64,128,128]{2,1,0:T(8,128)} fusion(f32[64,128,128]{2,1,0:T(8,128)} %get-tuple-element.471, pred[]{:T(512)S(6)} %compare.95, bf16[64,128,2048]{2,1,0:T(8,128)(2,1)} %reshape.449, bf16[2048,64,128]{2,1,0:T(8,128)(2,1)} %bitcast.129), kind=kOutput, calls=%fused_computation.6.clone.1 | convolution fusion | flops 4297064448 | bytes 75497472 | tf_op jit(solution)/shard_map/while/body/eval_jaxpr/qak,kqb->qab/dot_general | solution.py:58
  1460.2 4.2 collective-permute-start
  1464.4 3.1 copy.47
  1470.8 13.8 convert_bitcast_fusion.4
  1484.6 49.3 %reshape.449 = bf16[64,128,2048]{2,1,0:T(8,128)(2,1)} reshape(bf16[64,128,16,128]{3,2,1,0:T(8,128)(2,1)} %convert_bitcast_fusion.4) | data formatting | bytes 67108864 | tf_op jit(solution)/shard_map/while/body/eval_jaxpr/reshape | solution.py:44
  1533.9 15.5 convolution_convert_fusion.2
  1549.5 80.5 %select_add_fusion.2 = f32[64,128,128]{2,1,0:T(8,128)} fusion(f32[64,128,128]{2,1,0:T(8,128)} %get-tuple-element.471, pred[]{:T(512)S(6)} %compare.95, bf16[64,128,2048]{2,1,0:T(8,128)(2,1)} %reshape.449, bf16[2048,64,128]{2,1,0:T(8,128)(2,1)} %bitcast.129), kind=kOutput, calls=%fused_computation.6.clone.1 | convolution fusion | flops 4297064448 | bytes 75497472 | tf_op jit(solution)/shard_map/while/body/eval_jaxpr/qak,kqb->qab/dot_general | solution.py:58
  1631.6 3.1 copy.47
  1636.8 13.8 convert_bitcast_fusion.4
  1650.6 49.3 %reshape.449 = bf16[64,128,2048]{2,1,0:T(8,128)(2,1)} reshape(bf16[64,128,16,128]{3,2,1,0:T(8,128)(2,1)} %convert_bitcast_fusion.4) | data formatting | bytes 67108864 | tf_op jit(solution)/shard_map/while/body/eval_jaxpr/reshape | solution.py:44
  1699.9 15.5 convolution_convert_fusion.2
  1715.5 80.5 %select_add_fusion.2 = f32[64,128,128]{2,1,0:T(8,128)} fusion(f32[64,128,128]{2,1,0:T(8,128)} %get-tuple-element.471, pred[]{:T(512)S(6)} %compare.95, bf16[64,128,2048]{2,1,0:T(8,128)(2,1)} %reshape.449, bf16[2048,64,128]{2,1,0:T(8,128)(2,1)} %bitcast.129), kind=kOutput, calls=%fused_computation.6.clone.1 | convolution fusion | flops 4297064448 | bytes 75497472 | tf_op jit(solution)/shard_map/while/body/eval_jaxpr/qak,kqb->qab/dot_general | solution.py:58
  1797.6 3.1 copy.47
  1804.0 13.8 convert_bitcast_fusion.4
  1817.8 49.3 %reshape.449 = bf16[64,128,2048]{2,1,0:T(8,128)(2,1)} reshape(bf16[64,128,16,128]{3,2,1,0:T(8,128)(2,1)} %convert_bitcast_fusion.4) | data formatting | bytes 67108864 | tf_op jit(solution)/shard_map/while/body/eval_jaxpr/reshape | solution.py:44
  1867.1 15.5 convolution_convert_fusion.2
  1882.6 80.5 %select_add_fusion.2 = f32[64,128,128]{2,1,0:T(8,128)} fusion(f32[64,128,128]{2,1,0:T(8,128)} %get-tuple-element.471, pred[]{:T(512)S(6)} %compare.95, bf16[64,128,2048]{2,1,0:T(8,128)(2,1)} %reshape.449, bf16[2048,64,128]{2,1,0:T(8,128)(2,1)} %bitcast.129), kind=kOutput, calls=%fused_computation.6.clone.1 | convolution fusion | flops 4297064448 | bytes 75497472 | tf_op jit(solution)/shard_map/while/body/eval_jaxpr/qak,kqb->qab/dot_general | solution.py:58
  1963.7 15.6 convert_bitcast_fusion.1
  1979.3 23.4 %copy.17 = bf16[16,128,64,128]{3,2,1,0:T(8,128)(2,1)} copy(bf16[16,128,64,128]{3,2,0,1:T(8,128)(2,1)} %convert_bitcast_fusion.1) | data formatting | bytes 67108864 | tf_op jit(solution)/shard_map/convert_element_type | solution.py:57
  2002.7 15.6 convert_bitcast_fusion.2
  2018.3 47.5 %copy.16 = bf16[64,128,16,128]{1,3,2,0:T(8,128)(2,1)} copy(bf16[64,128,16,128]{3,0,2,1:T(8,128)(2,1)} %convert_bitcast_fusion.2) | data formatting | bytes 67108864 | tf_op jit(solution)/shard_map/convert_element_type | solution.py:44
  2065.8 78.4 %fusion.14 = f32[64,128,128]{2,1,0:T(8,128)} fusion(bf16[64,128,2048]{1,2,0:T(8,128)(2,1)} %bitcast.133, bf16[2048,64,128]{2,1,0:T(8,128)(2,1)} %bitcast.132), kind=kOutput, calls=%fused_computation.39 | convolution fusion | flops 4294967296 | bytes 71303168 | tf_op jit(solution)/shard_map/qak,kqb->qab/dot_general | solution.py:58
  2144.2 5.9 select_bitcast_fusion
  (160 shorter events, 36.0 us)
Async XLA Ops:
  7.2 616.6 %all-gather.3.cloned.1.call-start = ((), (), s32[]{:S(2)}) async-start(), calls=%async_computation | async-start | bytes 83886080 | tf_op jit(solution)/shard_map/all_gather | solution.py:8
  21.0 1.6 copy-start
  22.6 3.3 copy-start.3
  25.3 681.2 %collective-permute-start.8 = (bf16[64,128,128]{2,0,1:T(8,128)(2,1)}, bf16[64,128,128]{2,0,1:T(8,128)(2,1)}, u32[]{:S(2)}, u32[]{:S(2)}) collective-permute-start(bf16[64,128,128]{2,0,1:T(8,128)(2,1)} %bitcast.108), channel_id=1, source_target_pairs={{8,0},{16,8},{24,16},{0,24},{9,1},{17,9},{25,17},{1,25},{10,2},{18... | collective-permute-start | bytes 6291464 | tf_op jit(solution)/shard_map/ppermute | solution.py:29
  702.8 26.9 %collective-permute-start.4 = (bf16[64,128,128]{2,1,0:T(8,128)(2,1)}, bf16[64,128,128]{2,1,0:T(8,128)(2,1)}, u32[]{:S(2)}, u32[]{:S(2)}) collective-permute-start(bf16[64,128,128]{2,1,0:T(8,128)(2,1)} %select_convert_fusion), channel_id=1, source_target_pairs={{1,0},{2,1},{3,2},{4,3},{5,4},{6,5},{7,6},{0,7},{9,8},{10,9},{11,1... | collective-permute-start | bytes 6291464 | tf_op jit(solution)/shard_map/ppermute | solution.py:29
  709.7 23.9 %copy-start.2 = (s32[1,1,64]{2,1,0:T(1,128)S(1)}, s32[1,1,64]{2,1,0:T(1,128)}, u32[]{:S(2)}) copy-start(s32[1,1,64]{2,1,0:T(1,128)} %param.14) | copy-start | bytes 772
  709.7 29.3 %copy-start.5 = (s32[1,1,64]{2,1,0:T(1,128)S(1)}, s32[1,1,64]{2,1,0:T(1,128)}, u32[]{:S(2)}) copy-start(s32[1,1,64]{2,1,0:T(1,128)} %param.16) | copy-start | bytes 772
  709.7 71.6 %collective-permute-start.9 = (bf16[64,128,128]{2,0,1:T(8,128)(2,1)S(1)}, bf16[64,128,128]{2,0,1:T(8,128)(2,1)}, u32[]{:S(2)}, u32[]{:S(2)}) collective-permute-start(bf16[64,128,128]{2,0,1:T(8,128)(2,1)S(1)} %broadcast_select_fusion.1), channel_id=1, source_target_pairs={{16,0},{24,8},{0,16},{8,24},{17,1},{25,9},{1,17},{9,25},{18,2},{26... | collective-permute-start | bytes 6291464 | tf_op jit(solution)/shard_map/ppermute | solution.py:29
  732.9 49.9 %collective-permute-start.5 = (bf16[64,128,128]{2,1,0:T(8,128)(2,1)}, bf16[64,128,128]{2,1,0:T(8,128)(2,1)}, u32[]{:S(2)}, u32[]{:S(2)}) collective-permute-start(bf16[64,128,128]{2,1,0:T(8,128)(2,1)} %broadcast_select_fusion.3), channel_id=1, source_target_pairs={{2,0},{3,1},{4,2},{5,3},{6,4},{7,5},{0,6},{1,7},{10,8},{11,9},{12,... | collective-permute-start | bytes 6291464 | tf_op jit(solution)/shard_map/ppermute | solution.py:29
  733.5 6.0 collective-permute-start.10
  735.0 42.4 %collective-permute-start.6 = (s32[64]{0:T(128)S(1)}, s32[64]{0:T(128)S(1)}, u32[]{:S(2)}, u32[]{:S(2)}) collective-permute-start(s32[64]{0:T(128)S(1)} %bitcast_select_fusion), channel_id=1, source_target_pairs={{1,0},{2,1},{3,2},{4,3},{5,4},{6,5},{7,6},{0,7},{9,8},{10,9},{11,1... | collective-permute-start | bytes 776 | tf_op jit(solution)/shard_map/ppermute | solution.py:29
  739.6 38.7 %collective-permute-start.11 = (s32[64]{0:T(128)S(1)}, s32[64]{0:T(128)S(1)}, u32[]{:S(2)}, u32[]{:S(2)}) collective-permute-start(s32[64]{0:T(128)S(1)} %broadcast_select_fusion.5), channel_id=1, source_target_pairs={{16,0},{24,8},{0,16},{8,24},{17,1},{25,9},{1,17},{9,25},{18,2},{26... | collective-permute-start | bytes 776 | tf_op jit(solution)/shard_map/ppermute | solution.py:29
  777.4 3.8 collective-permute-start.7
  787.2 1176.4 %copy-start.4 = (s32[64]{0:T(128)S(1)}, s32[64]{0:T(128)}, u32[]{:S(2)}) copy-start(s32[64]{0:T(128)} %fusion.26) | copy-start | bytes 772
  789.0 170.3 %collective-permute-start = (bf16[64,128,128]{2,0,1:T(8,128)(2,1)S(1)}, bf16[64,128,128]{2,0,1:T(8,128)(2,1)}, u32[]{:S(2)}, u32[]{:S(2)}) collective-permute-start(bf16[64,128,128]{2,0,1:T(8,128)(2,1)S(1)} %copy.45), channel_id=1, source_target_pairs={{1,0},{2,1},{3,2},{4,3},{5,4},{6,5},{7,6},{0,7},{9,8},{10,9},{11,1... | collective-permute-start | bytes 6291464 | tf_op jit(solution)/shard_map/while/body/eval_jaxpr/ppermute | solution.py:29
  798.1 161.2 %collective-permute-start.2 = (bf16[64,128,128]{2,0,1:T(8,128)(2,1)}, bf16[64,128,128]{2,0,1:T(8,128)(2,1)}, u32[]{:S(2)}, u32[]{:S(2)}) collective-permute-start(bf16[64,128,128]{2,0,1:T(8,128)(2,1)} %copy.47), channel_id=1, source_target_pairs={{8,0},{16,8},{24,16},{0,24},{9,1},{17,9},{25,17},{1,25},{10,2},{18... | collective-permute-start | bytes 6291464 | tf_op jit(solution)/shard_map/while/body/eval_jaxpr/ppermute | solution.py:29
  799.6 159.7 %collective-permute-start.1 = (s32[64]{0:T(128)S(1)}, s32[64]{0:T(128)S(1)}, u32[]{:S(2)}, u32[]{:S(2)}) collective-permute-start(s32[64]{0:T(128)S(1)} %copy.46), channel_id=1, source_target_pairs={{1,0},{2,1},{3,2},{4,3},{5,4},{6,5},{7,6},{0,7},{9,8},{10,9},{11,1... | collective-permute-start | bytes 776 | tf_op jit(solution)/shard_map/while/body/eval_jaxpr/ppermute | solution.py:29
  799.6 159.7 %collective-permute-start.3 = (s32[64]{0:T(128)S(1)}, s32[64]{0:T(128)S(1)}, u32[]{:S(2)}, u32[]{:S(2)}) collective-permute-start(s32[64]{0:T(128)S(1)} %copy.48), channel_id=1, source_target_pairs={{8,0},{16,8},{24,16},{0,24},{9,1},{17,9},{25,17},{1,25},{10,2},{18... | collective-permute-start | bytes 776 | tf_op jit(solution)/shard_map/while/body/eval_jaxpr/ppermute | solution.py:29
  961.0 164.4 %collective-permute-start = (bf16[64,128,128]{2,0,1:T(8,128)(2,1)S(1)}, bf16[64,128,128]{2,0,1:T(8,128)(2,1)}, u32[]{:S(2)}, u32[]{:S(2)}) collective-permute-start(bf16[64,128,128]{2,0,1:T(8,128)(2,1)S(1)} %copy.45), channel_id=1, source_target_pairs={{1,0},{2,1},{3,2},{4,3},{5,4},{6,5},{7,6},{0,7},{9,8},{10,9},{11,1... | collective-permute-start | bytes 6291464 | tf_op jit(solution)/shard_map/while/body/eval_jaxpr/ppermute | solution.py:29
  964.1 161.3 %collective-permute-start.2 = (bf16[64,128,128]{2,0,1:T(8,128)(2,1)}, bf16[64,128,128]{2,0,1:T(8,128)(2,1)}, u32[]{:S(2)}, u32[]{:S(2)}) collective-permute-start(bf16[64,128,128]{2,0,1:T(8,128)(2,1)} %copy.47), channel_id=1, source_target_pairs={{8,0},{16,8},{24,16},{0,24},{9,1},{17,9},{25,17},{1,25},{10,2},{18... | collective-permute-start | bytes 6291464 | tf_op jit(solution)/shard_map/while/body/eval_jaxpr/ppermute | solution.py:29
  965.5 159.8 %collective-permute-start.1 = (s32[64]{0:T(128)S(1)}, s32[64]{0:T(128)S(1)}, u32[]{:S(2)}, u32[]{:S(2)}) collective-permute-start(s32[64]{0:T(128)S(1)} %copy.46), channel_id=1, source_target_pairs={{1,0},{2,1},{3,2},{4,3},{5,4},{6,5},{7,6},{0,7},{9,8},{10,9},{11,1... | collective-permute-start | bytes 776 | tf_op jit(solution)/shard_map/while/body/eval_jaxpr/ppermute | solution.py:29
  965.5 159.8 %collective-permute-start.3 = (s32[64]{0:T(128)S(1)}, s32[64]{0:T(128)S(1)}, u32[]{:S(2)}, u32[]{:S(2)}) collective-permute-start(s32[64]{0:T(128)S(1)} %copy.48), channel_id=1, source_target_pairs={{8,0},{16,8},{24,16},{0,24},{9,1},{17,9},{25,17},{1,25},{10,2},{18... | collective-permute-start | bytes 776 | tf_op jit(solution)/shard_map/while/body/eval_jaxpr/ppermute | solution.py:29
  1126.9 165.6 %collective-permute-start = (bf16[64,128,128]{2,0,1:T(8,128)(2,1)S(1)}, bf16[64,128,128]{2,0,1:T(8,128)(2,1)}, u32[]{:S(2)}, u32[]{:S(2)}) collective-permute-start(bf16[64,128,128]{2,0,1:T(8,128)(2,1)S(1)} %copy.45), channel_id=1, source_target_pairs={{1,0},{2,1},{3,2},{4,3},{5,4},{6,5},{7,6},{0,7},{9,8},{10,9},{11,1... | collective-permute-start | bytes 6291464 | tf_op jit(solution)/shard_map/while/body/eval_jaxpr/ppermute | solution.py:29
  1130.1 162.4 %collective-permute-start.2 = (bf16[64,128,128]{2,0,1:T(8,128)(2,1)}, bf16[64,128,128]{2,0,1:T(8,128)(2,1)}, u32[]{:S(2)}, u32[]{:S(2)}) collective-permute-start(bf16[64,128,128]{2,0,1:T(8,128)(2,1)} %copy.47), channel_id=1, source_target_pairs={{8,0},{16,8},{24,16},{0,24},{9,1},{17,9},{25,17},{1,25},{10,2},{18... | collective-permute-start | bytes 6291464 | tf_op jit(solution)/shard_map/while/body/eval_jaxpr/ppermute | solution.py:29
  1131.6 160.9 %collective-permute-start.1 = (s32[64]{0:T(128)S(1)}, s32[64]{0:T(128)S(1)}, u32[]{:S(2)}, u32[]{:S(2)}) collective-permute-start(s32[64]{0:T(128)S(1)} %copy.46), channel_id=1, source_target_pairs={{1,0},{2,1},{3,2},{4,3},{5,4},{6,5},{7,6},{0,7},{9,8},{10,9},{11,1... | collective-permute-start | bytes 776 | tf_op jit(solution)/shard_map/while/body/eval_jaxpr/ppermute | solution.py:29
  1131.6 160.9 %collective-permute-start.3 = (s32[64]{0:T(128)S(1)}, s32[64]{0:T(128)S(1)}, u32[]{:S(2)}, u32[]{:S(2)}) collective-permute-start(s32[64]{0:T(128)S(1)} %copy.48), channel_id=1, source_target_pairs={{8,0},{16,8},{24,16},{0,24},{9,1},{17,9},{25,17},{1,25},{10,2},{18... | collective-permute-start | bytes 776 | tf_op jit(solution)/shard_map/while/body/eval_jaxpr/ppermute | solution.py:29
  1294.1 164.4 %collective-permute-start = (bf16[64,128,128]{2,0,1:T(8,128)(2,1)S(1)}, bf16[64,128,128]{2,0,1:T(8,128)(2,1)}, u32[]{:S(2)}, u32[]{:S(2)}) collective-permute-start(bf16[64,128,128]{2,0,1:T(8,128)(2,1)S(1)} %copy.45), channel_id=1, source_target_pairs={{1,0},{2,1},{3,2},{4,3},{5,4},{6,5},{7,6},{0,7},{9,8},{10,9},{11,1... | collective-permute-start | bytes 6291464 | tf_op jit(solution)/shard_map/while/body/eval_jaxpr/ppermute | solution.py:29
  1297.3 161.3 %collective-permute-start.2 = (bf16[64,128,128]{2,0,1:T(8,128)(2,1)}, bf16[64,128,128]{2,0,1:T(8,128)(2,1)}, u32[]{:S(2)}, u32[]{:S(2)}) collective-permute-start(bf16[64,128,128]{2,0,1:T(8,128)(2,1)} %copy.47), channel_id=1, source_target_pairs={{8,0},{16,8},{24,16},{0,24},{9,1},{17,9},{25,17},{1,25},{10,2},{18... | collective-permute-start | bytes 6291464 | tf_op jit(solution)/shard_map/while/body/eval_jaxpr/ppermute | solution.py:29
  1298.7 159.9 %collective-permute-start.1 = (s32[64]{0:T(128)S(1)}, s32[64]{0:T(128)S(1)}, u32[]{:S(2)}, u32[]{:S(2)}) collective-permute-start(s32[64]{0:T(128)S(1)} %copy.46), channel_id=1, source_target_pairs={{1,0},{2,1},{3,2},{4,3},{5,4},{6,5},{7,6},{0,7},{9,8},{10,9},{11,1... | collective-permute-start | bytes 776 | tf_op jit(solution)/shard_map/while/body/eval_jaxpr/ppermute | solution.py:29
  1298.7 159.9 %collective-permute-start.3 = (s32[64]{0:T(128)S(1)}, s32[64]{0:T(128)S(1)}, u32[]{:S(2)}, u32[]{:S(2)}) collective-permute-start(s32[64]{0:T(128)S(1)} %copy.48), channel_id=1, source_target_pairs={{8,0},{16,8},{24,16},{0,24},{9,1},{17,9},{25,17},{1,25},{10,2},{18... | collective-permute-start | bytes 776 | tf_op jit(solution)/shard_map/while/body/eval_jaxpr/ppermute | solution.py:29
  1460.2 169.8 %collective-permute-start = (bf16[64,128,128]{2,0,1:T(8,128)(2,1)S(1)}, bf16[64,128,128]{2,0,1:T(8,128)(2,1)}, u32[]{:S(2)}, u32[]{:S(2)}) collective-permute-start(bf16[64,128,128]{2,0,1:T(8,128)(2,1)S(1)} %copy.45), channel_id=1, source_target_pairs={{1,0},{2,1},{3,2},{4,3},{5,4},{6,5},{7,6},{0,7},{9,8},{10,9},{11,1... | collective-permute-start | bytes 6291464 | tf_op jit(solution)/shard_map/while/body/eval_jaxpr/ppermute | solution.py:29
  1467.5 162.5 %collective-permute-start.2 = (bf16[64,128,128]{2,0,1:T(8,128)(2,1)}, bf16[64,128,128]{2,0,1:T(8,128)(2,1)}, u32[]{:S(2)}, u32[]{:S(2)}) collective-permute-start(bf16[64,128,128]{2,0,1:T(8,128)(2,1)} %copy.47), channel_id=1, source_target_pairs={{8,0},{16,8},{24,16},{0,24},{9,1},{17,9},{25,17},{1,25},{10,2},{18... | collective-permute-start | bytes 6291464 | tf_op jit(solution)/shard_map/while/body/eval_jaxpr/ppermute | solution.py:29
  1469.0 160.9 %collective-permute-start.1 = (s32[64]{0:T(128)S(1)}, s32[64]{0:T(128)S(1)}, u32[]{:S(2)}, u32[]{:S(2)}) collective-permute-start(s32[64]{0:T(128)S(1)} %copy.46), channel_id=1, source_target_pairs={{1,0},{2,1},{3,2},{4,3},{5,4},{6,5},{7,6},{0,7},{9,8},{10,9},{11,1... | collective-permute-start | bytes 776 | tf_op jit(solution)/shard_map/while/body/eval_jaxpr/ppermute | solution.py:29
  1469.0 160.9 %collective-permute-start.3 = (s32[64]{0:T(128)S(1)}, s32[64]{0:T(128)S(1)}, u32[]{:S(2)}, u32[]{:S(2)}) collective-permute-start(s32[64]{0:T(128)S(1)} %copy.48), channel_id=1, source_target_pairs={{8,0},{16,8},{24,16},{0,24},{9,1},{17,9},{25,17},{1,25},{10,2},{18... | collective-permute-start | bytes 776 | tf_op jit(solution)/shard_map/while/body/eval_jaxpr/ppermute | solution.py:29
  1631.6 164.4 %collective-permute-start = (bf16[64,128,128]{2,0,1:T(8,128)(2,1)S(1)}, bf16[64,128,128]{2,0,1:T(8,128)(2,1)}, u32[]{:S(2)}, u32[]{:S(2)}) collective-permute-start(bf16[64,128,128]{2,0,1:T(8,128)(2,1)S(1)} %copy.45), channel_id=1, source_target_pairs={{1,0},{2,1},{3,2},{4,3},{5,4},{6,5},{7,6},{0,7},{9,8},{10,9},{11,1... | collective-permute-start | bytes 6291464 | tf_op jit(solution)/shard_map/while/body/eval_jaxpr/ppermute | solution.py:29
  1634.7 161.3 %collective-permute-start.2 = (bf16[64,128,128]{2,0,1:T(8,128)(2,1)}, bf16[64,128,128]{2,0,1:T(8,128)(2,1)}, u32[]{:S(2)}, u32[]{:S(2)}) collective-permute-start(bf16[64,128,128]{2,0,1:T(8,128)(2,1)} %copy.47), channel_id=1, source_target_pairs={{8,0},{16,8},{24,16},{0,24},{9,1},{17,9},{25,17},{1,25},{10,2},{18... | collective-permute-start | bytes 6291464 | tf_op jit(solution)/shard_map/while/body/eval_jaxpr/ppermute | solution.py:29
  1636.1 159.8 %collective-permute-start.1 = (s32[64]{0:T(128)S(1)}, s32[64]{0:T(128)S(1)}, u32[]{:S(2)}, u32[]{:S(2)}) collective-permute-start(s32[64]{0:T(128)S(1)} %copy.46), channel_id=1, source_target_pairs={{1,0},{2,1},{3,2},{4,3},{5,4},{6,5},{7,6},{0,7},{9,8},{10,9},{11,1... | collective-permute-start | bytes 776 | tf_op jit(solution)/shard_map/while/body/eval_jaxpr/ppermute | solution.py:29
  1636.1 159.8 %collective-permute-start.3 = (s32[64]{0:T(128)S(1)}, s32[64]{0:T(128)S(1)}, u32[]{:S(2)}, u32[]{:S(2)}) collective-permute-start(s32[64]{0:T(128)S(1)} %copy.48), channel_id=1, source_target_pairs={{8,0},{16,8},{24,16},{0,24},{9,1},{17,9},{25,17},{1,25},{10,2},{18... | collective-permute-start | bytes 776 | tf_op jit(solution)/shard_map/while/body/eval_jaxpr/ppermute | solution.py:29
  1797.6 165.6 %collective-permute-start = (bf16[64,128,128]{2,0,1:T(8,128)(2,1)S(1)}, bf16[64,128,128]{2,0,1:T(8,128)(2,1)}, u32[]{:S(2)}, u32[]{:S(2)}) collective-permute-start(bf16[64,128,128]{2,0,1:T(8,128)(2,1)S(1)} %copy.45), channel_id=1, source_target_pairs={{1,0},{2,1},{3,2},{4,3},{5,4},{6,5},{7,6},{0,7},{9,8},{10,9},{11,1... | collective-permute-start | bytes 6291464 | tf_op jit(solution)/shard_map/while/body/eval_jaxpr/ppermute | solution.py:29
  1800.7 162.4 %collective-permute-start.2 = (bf16[64,128,128]{2,0,1:T(8,128)(2,1)}, bf16[64,128,128]{2,0,1:T(8,128)(2,1)}, u32[]{:S(2)}, u32[]{:S(2)}) collective-permute-start(bf16[64,128,128]{2,0,1:T(8,128)(2,1)} %copy.47), channel_id=1, source_target_pairs={{8,0},{16,8},{24,16},{0,24},{9,1},{17,9},{25,17},{1,25},{10,2},{18... | collective-permute-start | bytes 6291464 | tf_op jit(solution)/shard_map/while/body/eval_jaxpr/ppermute | solution.py:29
  1802.2 160.9 %collective-permute-start.1 = (s32[64]{0:T(128)S(1)}, s32[64]{0:T(128)S(1)}, u32[]{:S(2)}, u32[]{:S(2)}) collective-permute-start(s32[64]{0:T(128)S(1)} %copy.46), channel_id=1, source_target_pairs={{1,0},{2,1},{3,2},{4,3},{5,4},{6,5},{7,6},{0,7},{9,8},{10,9},{11,1... | collective-permute-start | bytes 776 | tf_op jit(solution)/shard_map/while/body/eval_jaxpr/ppermute | solution.py:29
  1802.2 160.9 %collective-permute-start.3 = (s32[64]{0:T(128)S(1)}, s32[64]{0:T(128)S(1)}, u32[]{:S(2)}, u32[]{:S(2)}) collective-permute-start(s32[64]{0:T(128)S(1)} %copy.48), channel_id=1, source_target_pairs={{8,0},{16,8},{24,16},{0,24},{9,1},{17,9},{25,17},{1,25},{10,2},{18... | collective-permute-start | bytes 776 | tf_op jit(solution)/shard_map/while/body/eval_jaxpr/ppermute | solution.py:29
  2065.8 78.4 %copy-start.1 = (pred[64]{0:T(512)(128)(4,1)S(1)}, pred[64]{0:T(512)(128)(4,1)}, u32[]{:S(2)}) copy-start(pred[64]{0:T(512)(128)(4,1)} %iota_compare_fusion.4) | copy-start | bytes 196
Sparse Core Ops, SparseCore 0:
  21.2 602.5 all-gather.2
